TPU v7x, 512 devices: a whole 4x4x16 slice. The times are simulated.
512 devices in a mesh: tok: 64 (over y_lo, z, core), row: 8 (over y_hi, x).
Axes of the slice: x: 4, y: 4 (y_hi: 2, y_lo: 2; y = y_hi * 2 + y_lo), z: 16, core: 2. Of those that a mesh axis runs over, the one named last changes fastest.
Arguments:
- calib: bfloat16 [8192, 4096], P('row', 'tok'), may hold values from -8 to 8
- base_weight: bfloat16 [8192, 4096], P('tok', 'row'), may hold values from -6 to 6
- keep_blocks: int32 [64, 16], replicated, may hold values from 0 to 31, all different within a row
Outputs:
- refined: bfloat16 [8192, 4096], P('tok', 'row')
Inputs may be any that keep to these rules, and one draw needn't show every extreme that they name: `keep_blocks`: each row lists 16 different block columns, and every block column is listed in some row.
All inputs are finite; a program needn't handle non-finite values.
Results may differ from a plain program's by a relative error of at most 0.0085.
Values may be sent and summed in bfloat16 or wider, within the bound.
No kernel may reach another device: no remote copies, remote signals or barrier semaphores. Data moves between devices by JAX's collectives and lax.ppermute only.
A program may use at most 64 MiB of HBM per device.

v0:
```python
import jax
import jax.numpy as jnp
from jax import lax
from jax.sharding import PartitionSpec as P

BLOCK = 128


def block_table(keep_blocks, ncols):
    labels = jnp.arange(ncols, dtype=jnp.int32)
    hits = (keep_blocks[:, :, None] == labels[None, None, :]).astype(jnp.float32)
    return jnp.sum(hits, axis=1)


def selector(first, count, nblocks):
    ids = (first + jnp.arange(count, dtype=jnp.int32)) // BLOCK
    return (ids[:, None] == jnp.arange(nblocks, dtype=jnp.int32)[None, :]).astype(jnp.float32)


def residual_product(diff, gram_cols):
    return jnp.dot(
        lax.all_gather(diff, "row", axis=1, tiled=True),
        gram_cols,
        preferred_element_type=jnp.float32,
    )


def on_device(calib, base_weight, keep_blocks):
    tok_pos = lax.axis_index("tok")
    row_pos = lax.axis_index("row")
    rows = base_weight.shape[0]
    cols = base_weight.shape[1]
    width = cols * lax.axis_size("row")
    tokens = calib.shape[0] * lax.axis_size("row")
    block_map = block_table(keep_blocks, width // BLOCK)
    row_sel = selector(tok_pos * rows, rows, block_map.shape[0])
    col_sel = selector(row_pos * cols, cols, block_map.shape[1])
    row_map = jnp.dot(row_sel, block_map)
    keep_local = jnp.dot(row_map, col_sel.T)
    base_float = base_weight.astype(jnp.float32)
    weight = (keep_local * base_float).astype(jnp.bfloat16)
    partial_value = lax.dot_general(
        calib,
        lax.all_gather(calib, "tok", axis=1, tiled=True),
        (((0,), (0,)), ((), ())),
        preferred_element_type=jnp.float32,
    )
    summed = lax.psum_scatter(partial_value, "row", scatter_dimension=1, tiled=True)
    gram_block = (summed / tokens).astype(jnp.bfloat16)
    gram_cols = lax.all_gather(gram_block, "tok", axis=0, tiled=True)
    diff = (weight.astype(jnp.float32) - base_float).astype(jnp.bfloat16)
    grad = residual_product(diff, gram_cols)
    weight = (weight.astype(jnp.float32) - 0.25 * keep_local * grad).astype(jnp.bfloat16)
    diff = (weight.astype(jnp.float32) - base_float).astype(jnp.bfloat16)
    grad = residual_product(diff, gram_cols)
    weight = (weight.astype(jnp.float32) - 0.25 * keep_local * grad).astype(jnp.bfloat16)
    return weight


def solution(mesh):
    return jax.shard_map(
        on_device,
        mesh=mesh,
        in_specs=(P("row", "tok"), P("tok", "row"), P()),
        out_specs=P("tok", "row"),
        check_vma=False,
    )
```

profile of v0, /device:TPU:2, one launch (start us, length us, event | category | flops | bytes accessed | tf_op | source)
XLA Modules:
  0.0 499.5 jit_solution(11192664810128790291)
XLA Ops:
  6.5 0.0 all-gather.7.cloned.1.call-start
  6.5 0.7 all-gather.7.cloned.1.call-update
  7.3 0.0 copy-start.1
  7.3 0.0 copy-start
  7.3 0.0 reduce-scatter.2.cloned.1.call-start
  7.3 135.7 %all-gather.7.cloned.1.call-done = bf16[1024,4096]{0,1:T(8,128)(2,1)} async-done(((bf16[1024,64]{0,1:T(8,128)(2,1)}), bf16[1024,4096]{0,1:T(8,128)(2,1)}) %all-gather.7.cloned.1.call-update) | async-done | bytes 8388624 | tf_op jit(solution)/shard_map/all_gather | solution.py:44
  143.0 7.2 %fusion.17 = f32[64,4096]{1,0:T(8,128)} fusion(bf16[1024,64]{0,1:T(8,128)(2,1)} %param.3, bf16[1024,4096]{0,1:T(8,128)(2,1)} %all-gather.7.cloned.1.call-done), kind=kOutput, calls=%fused_computation.35 | convolution fusion | flops 536870912 | bytes 9568256 | tf_op jit(solution)/shard_map/dot_general | solution.py:42
  150.2 0.0 reduce-scatter.2.cloned.1.call-update
  150.2 0.0 all-gather.5.cloned.1.call-start
  150.3 0.0 copy-done.1
  150.4 0.0 copy-done
  150.4 1.0 fusion.9
  151.4 0.0 all-gather.5.cloned.1.call-update
  151.4 0.0 all-gather.9.cloned.1.call-start
  151.5 81.9 %reduce-scatter.2.cloned.1.call-done = f32[64,512]{1,0:T(8,128)} async-done(((f32[64,4096]{1,0:T(8,128)}), f32[64,512]{1,0:T(8,128)}) %reduce-scatter.2.cloned.1.call-update) | async-done | bytes 131088 | tf_op jit(solution)/shard_map/reduce_scatter | solution.py:48
  233.3 1.5 multiply_convert_fusion
  234.9 0.0 all-gather.9.cloned.1.call-update
  234.9 0.0 all-gather.11.cloned.1.call-start
  234.9 64.8 %all-gather.5.cloned.1.call-done = bf16[128,4096]{1,0:T(8,128)(2,1)} async-done(((bf16[128,512]{1,0:T(8,128)(2,1)}), bf16[128,4096]{1,0:T(8,128)(2,1)}) %all-gather.5.cloned.1.call-update) | async-done | bytes 1048592 | tf_op jit(solution)/shard_map/all_gather | solution.py:22
  299.7 126.0 %all-gather.9.cloned.1.call-done = bf16[4096,512]{1,0:T(8,128)(2,1)} async-done(((bf16[64,512]{1,0:T(8,128)(2,1)}), bf16[4096,512]{1,0:T(8,128)(2,1)}) %all-gather.9.cloned.1.call-update) | async-done | bytes 4194320 | tf_op jit(solution)/shard_map/all_gather | solution.py:50
  425.7 3.9 fusion.10
  429.7 0.0 all-gather.11.cloned.1.call-update
  429.7 59.4 %all-gather.11.cloned.1.call-done = bf16[128,4096]{1,0:T(8,128)(2,1)} async-done(((bf16[128,512]{1,0:T(8,128)(2,1)}), bf16[128,4096]{1,0:T(8,128)(2,1)}) %all-gather.11.cloned.1.call-update) | async-done | bytes 1048592 | tf_op jit(solution)/shard_map/all_gather | solution.py:22
  489.1 3.9 fusion.4
  (3 shorter events, 0.1 us)
Async XLA Ops:
  6.5 136.5 %all-gather.7.cloned.1.call-start = ((), (), s32[]{:S(2)}) async-start(), calls=%async_computation.2 | async-start | bytes 8519680 | tf_op jit(solution)/shard_map/all_gather | solution.py:44
  7.3 143.1 %copy-start.1 = (s32[64,16]{0,1:T(8,128)S(1)}, s32[64,16]{0,1:T(8,128)}, u32[]{:S(2)}) copy-start(s32[64,16]{0,1:T(8,128)} %param.5) | copy-start | bytes 12292
  7.3 143.1 %copy-start = (bf16[128,512]{1,0:T(8,128)(2,1)S(1)}, bf16[128,512]{1,0:T(8,128)(2,1)}, u32[]{:S(2)}) copy-start(bf16[128,512]{1,0:T(8,128)(2,1)} %param.4) | copy-start | bytes 393220
  7.3 226.0 %reduce-scatter.2.cloned.1.call-start = ((), (), s32[]{:S(2)}) async-start(), calls=%async_computation.3 | async-start | bytes 1179648 | tf_op jit(solution)/shard_map/reduce_scatter | solution.py:48
  150.2 149.5 %all-gather.5.cloned.1.call-start = ((), (), s32[]{:S(2)}) async-start(), calls=%async_computation.1 | async-start | bytes 1179648 | tf_op jit(solution)/shard_map/all_gather | solution.py:22
  151.4 274.3 %all-gather.9.cloned.1.call-start = ((), (), s32[]{:S(2)}) async-start(), calls=%async_computation.4 | async-start | bytes 4259840 | tf_op jit(solution)/shard_map/all_gather | solution.py:50
  234.9 254.2 %all-gather.11.cloned.1.call-start = ((), (), s32[]{:S(2)}) async-start(), calls=%async_computation.5 | async-start | bytes 1179648 | tf_op jit(solution)/shard_map/all_gather | solution.py:22
Sparse Core Ops, SparseCore 0:
  9.5 133.4 all-gather.6
  150.3 82.9 reduce-scatter.1
  236.8 62.8 all-gather.4
  301.9 123.7 all-gather.8
  429.8 59.2 all-gather.10
where the time goes:
time: 500 us
  waiting for transfers between devices  469 us (94%)
  matrix products  16 us (3%)
  between operations  13.2 us (3%)
    all_gather x1, waiting for transfers between devices, on_device(): lax.all_gather(calib, 'tok', axis=1, tiled=True)  136 us
    all_gather x1, waiting for transfers between devices, on_device(): gram_cols = lax.all_gather(gram_block, 'tok', axis=0, tiled=True)  126 us
    all_gather x2, waiting for transfers between devices, residual_product(): lax.all_gather(diff, 'row', axis=1, tiled=True)  124 us
    reduce_scatter x1, waiting for transfers between devices, on_device(): lax.psum_scatter(partial_value, 'row', scatter_dimension=1, tiled=True)  81.9 us
  transfers between devices with their start and end apart: 5, of which 5 were waited for; matrix products, arithmetic and copies ran while one was open for 1% of the time, Pallas kernels for 0%

commit v1 on v0

--- a/solution.py
+++ b/solution.py
@@ -4,6 +4,11 @@
 from jax.sharding import PartitionSpec as P
 
 BLOCK = 128
+
+
+def gather_over(array, axis, along):
+    sent = jnp.stack([array] * lax.axis_size(axis))
+    return jnp.concatenate(lax.all_to_all(sent, axis, 0, 0), axis=along)
 
 
 def block_table(keep_blocks, ncols):
@@ -18,11 +23,7 @@
 
 
 def residual_product(diff, gram_cols):
-    return jnp.dot(
-        lax.all_gather(diff, "row", axis=1, tiled=True),
-        gram_cols,
-        preferred_element_type=jnp.float32,
-    )
+    return jnp.dot(gather_over(diff, "row", 1), gram_cols, preferred_element_type=jnp.float32)
 
 
 def on_device(calib, base_weight, keep_blocks):

time: 500 us -> 398 us (0.80)
  the two profiles are of different devices: /device:TPU:2 before, /device:TPU:1 now
where the time goes in v1:
time: 398 us
  waiting for transfers between devices  326 us (82%)
  blocking collectives  41.9 us (11%)
  matrix products  14.2 us (4%)
  between operations  13.2 us (3%)
    all_gather x1, waiting for transfers between devices, on_device(): lax.all_gather(calib, 'tok', axis=1, tiled=True)  137 us
    all_gather x1, waiting for transfers between devices, on_device(): gram_cols = lax.all_gather(gram_block, 'tok', axis=0, tiled=True)  107 us
    reduce_scatter x1, waiting for transfers between devices, on_device(): lax.psum_scatter(partial_value, 'row', scatter_dimension=1, tiled=True)  81.3 us
    all_to_all x2, blocking collectives, gather_over(): return jnp.concatenate(lax.all_to_all(sent, axis, 0, 0), axis=along)  41.9 us
  transfers between devices with their start and end apart: 3, of which 3 were waited for; matrix products, arithmetic and copies ran while one was open for 0% of the time, Pallas kernels for 0%

profile of v1, /device:TPU:1, one launch (start us, length us, event | category | flops | bytes accessed | tf_op | source)
XLA Modules:
  0.0 397.8 jit_solution(9340456343952404879)
XLA Ops:
  6.5 0.0 all-gather.3.cloned.1.call-start
  6.5 0.7 all-gather.3.cloned.1.call-update
  7.3 0.0 copy-start.1
  7.3 0.0 copy-start
  7.3 0.0 reduce-scatter.2.cloned.1.call-start
  7.3 136.8 %all-gather.3.cloned.1.call-done = bf16[1024,4096]{0,1:T(8,128)(2,1)} async-done(((bf16[1024,64]{0,1:T(8,128)(2,1)}), bf16[1024,4096]{0,1:T(8,128)(2,1)}) %all-gather.3.cloned.1.call-update) | async-done | bytes 8388624 | tf_op jit(solution)/shard_map/all_gather | solution.py:45
  144.1 7.2 %fusion.17 = f32[64,4096]{1,0:T(8,128)} fusion(bf16[1024,64]{0,1:T(8,128)(2,1)} %param.3, bf16[1024,4096]{0,1:T(8,128)(2,1)} %all-gather.3.cloned.1.call-done), kind=kOutput, calls=%fused_computation.35 | convolution fusion | flops 536870912 | bytes 9568256 | tf_op jit(solution)/shard_map/dot_general | solution.py:43
  151.3 0.0 reduce-scatter.2.cloned.1.call-update
  151.3 0.0 all-gather.5.cloned.1.call-start
  151.3 81.3 %reduce-scatter.2.cloned.1.call-done = f32[64,512]{1,0:T(8,128)} async-done(((f32[64,4096]{1,0:T(8,128)}), f32[64,512]{1,0:T(8,128)}) %reduce-scatter.2.cloned.1.call-update) | async-done | bytes 131088 | tf_op jit(solution)/shard_map/reduce_scatter | solution.py:49
  232.6 1.5 multiply_convert_fusion
  234.1 0.0 all-gather.5.cloned.1.call-update
  234.2 0.0 copy-done.1
  234.3 0.0 copy-done
  234.3 0.5 fusion.9
  234.7 0.1 copy.8
  234.9 0.1 stack.4
  235.0 18.6 %all_to_all.10 = bf16[8,128,512]{1,2,0:T(8,128)(2,1)S(1)} all-to-all(bf16[8,128,512]{1,2,0:T(8,128)(2,1)S(1)} %stack.4), channel_id=1, replica_groups=mesh['tok'=64,'row'=8] {'row'}, dimensions={0} | all-to-all | bytes 2097152 | tf_op jit(solution)/shard_map/all_to_all | solution.py:11
  253.6 107.5 %all-gather.5.cloned.1.call-done = bf16[4096,512]{1,0:T(8,128)(2,1)} async-done(((bf16[64,512]{1,0:T(8,128)(2,1)}), bf16[4096,512]{1,0:T(8,128)(2,1)}) %all-gather.5.cloned.1.call-update) | async-done | bytes 4194320 | tf_op jit(solution)/shard_map/all_gather | solution.py:51
  361.1 2.9 fusion.10
  364.0 0.1 copy.9
  364.2 0.1 stack.5
  364.3 23.3 %all_to_all.11 = bf16[8,128,512]{1,2,0:T(8,128)(2,1)S(1)} all-to-all(bf16[8,128,512]{1,2,0:T(8,128)(2,1)S(1)} %stack.5), channel_id=1, replica_groups=mesh['tok'=64,'row'=8] {'row'}, dimensions={0} | all-to-all | bytes 2097152 | tf_op jit(solution)/shard_map/all_to_all | solution.py:11
  387.6 3.6 fusion.4
  (3 shorter events, 0.1 us)
Async XLA Ops:
  6.5 137.6 %all-gather.3.cloned.1.call-start = ((), (), s32[]{:S(2)}) async-start(), calls=%async_computation.3 | async-start | bytes 8519680 | tf_op jit(solution)/shard_map/all_gather | solution.py:45
  7.3 227.0 %copy-start.1 = (s32[64,16]{0,1:T(8,128)S(1)}, s32[64,16]{0,1:T(8,128)}, u32[]{:S(2)}) copy-start(s32[64,16]{0,1:T(8,128)} %param.5) | copy-start | bytes 12292
  7.3 227.0 %copy-start = (bf16[128,512]{1,0:T(8,128)(2,1)S(1)}, bf16[128,512]{1,0:T(8,128)(2,1)}, u32[]{:S(2)}) copy-start(bf16[128,512]{1,0:T(8,128)(2,1)} %param.4) | copy-start | bytes 393220
  7.3 225.3 %reduce-scatter.2.cloned.1.call-start = ((), (), s32[]{:S(2)}) async-start(), calls=%async_computation.4 | async-start | bytes 1179648 | tf_op jit(solution)/shard_map/reduce_scatter | solution.py:49
  151.3 209.8 %all-gather.5.cloned.1.call-start = ((), (), s32[]{:S(2)}) async-start(), calls=%async_computation.5 | async-start | bytes 4259840 | tf_op jit(solution)/shard_map/all_gather | solution.py:51
Sparse Core Ops, SparseCore 0:
  9.5 134.5 all-gather.2
  151.4 81.1 reduce-scatter.1
  235.0 126.0 all-gather.4
